TPU v7x, 256 devices: a whole 4x4x8 slice. The times are simulated.
256 devices in a mesh: grp: 8 (over x, core), vocab: 32 (over y, z).
Axes of the slice: x: 4, y: 4, z: 8, core: 2. Of those that a mesh axis runs over, the one named last changes fastest.
Arguments:
- hidden: bfloat16 [1024, 16384], P('grp', 'vocab'), may hold values from -6 to 6
- flags: int32 [1024, 1], P('grp'), may hold values from 0 to 8; in each aligned block of 128 rows (0 to 127, 128 to 255, ...) at most 16 rows name the same one
- targets: int32 [1024], P('grp'), may hold values from 0 to 65535
- head: bfloat16 [16384, 65536], P('grp', 'vocab'), may hold values from -0.140625 to 0.140625
- lengths: int32 [8, 8], P('grp'), may hold values from 1 to 64, 128 in all within a row
Outputs:
- token_scores: float32 [1024], P('grp')
- doc_scores: float32 [8, 8], P('grp')
Inputs may be any that keep to these rules, and one draw needn't show every extreme that they name: `flags`: A value below 8 names the scorer group of a scored row. Within the 128 rows of one shard no value occurs more than 16 times, and in every draw some value occurs exactly 16 times in some shard.
All inputs are finite; a program needn't handle non-finite values.
Results may differ from a plain program's by a relative error of at most 0.0003.
Values may be sent and summed in bfloat16 or wider, within the bound.
A program may use at most 128 MiB of HBM per device.

v0:
```python
import jax
import jax.numpy as jnp
from jax import lax
from jax.sharding import PartitionSpec as P


def combined_all(part, axis, combine):
    gathered = jax.tree.map(lambda a: lax.all_gather(a, axis), part)

    def take(source):
        return jax.tree.map(lambda a: lax.dynamic_index_in_dim(a, source, 0, False), gathered)

    return lax.fori_loop(
        1, lax.axis_size(axis), lambda source, state: combine(state, take(source)), take(0)
    )


def slot_table(flag_col, groups, capacity, shard_rows):
    values = jnp.arange(groups + 1, dtype=jnp.int32)
    onehot = (flag_col[:, None] == values[None, :]).astype(jnp.int32)
    ranking = jnp.sum((jnp.cumsum(onehot, axis=0) - 1) * onehot, axis=1)
    where_to = jnp.where(flag_col < groups, flag_col * capacity + ranking, groups * capacity)
    table = jnp.full((groups * capacity + 1,), -1, jnp.int32)
    table = table.at[where_to].set(jnp.arange(shard_rows, dtype=jnp.int32))
    return table[: groups * capacity]


def combine_stats(left, right):
    row_max = jnp.maximum(left[0], right[0])
    left_gap = left[0] - row_max
    right_gap = right[0] - row_max
    left_fac = jnp.exp(left_gap)
    right_fac = jnp.exp(right_gap)
    row_total = left_fac * left[1] + right_fac * right[1]
    first_mom = left_fac * (left[2] + left_gap * left[1]) + right_fac * (
        right[2] + right_gap * right[1]
    )
    second_mom = left_fac * (left[3] + 2.0 * left_gap * left[2] + left_gap * left_gap * left[1])
    second_mom = second_mom + right_fac * (
        right[3] + 2.0 * right_gap * right[2] + right_gap * right_gap * right[1]
    )
    return (row_max, row_total, first_mom, second_mom)


def local_stats(logits, target_ids, columns, axis):
    row_max = jnp.max(logits, axis=axis)
    shifted = logits - jnp.expand_dims(row_max, axis)
    scaled = jnp.exp(shifted)
    row_total = jnp.sum(scaled, axis=axis)
    first_mom = jnp.sum(scaled * shifted, axis=axis)
    second_mom = jnp.sum(scaled * shifted * shifted, axis=axis)
    is_target = target_ids[:, None] == columns[None, :]
    target_val = jnp.sum(jnp.where(is_target, logits, jnp.float32(0.0)), axis=axis)
    return (row_max, row_total, first_mom, second_mom, target_val)


def final_scores(target_ids, row_max, row_total, first_mom, second_mom, target_val):
    mean_shift = first_mom / row_total
    row_var = second_mom / row_total - mean_shift * mean_shift
    return jnp.where(
        target_ids >= 0,
        (target_val - row_max - mean_shift) / jnp.sqrt(jnp.maximum(row_var, 1.0)),
        jnp.float32(0.0),
    )


def shards(hidden, flags, targets, head, lengths):
    groups = lax.axis_size("grp")
    shard_rows = hidden.shape[0]
    capacity = shard_rows // groups
    vocab_dev = head.shape[1]
    my_vocab = lax.axis_index("vocab")
    flag_col = flags[:, 0]
    table = slot_table(flag_col, groups, capacity, shard_rows)
    is_live = table >= 0
    safe_rows = jnp.maximum(table, 0)
    pieces = jnp.where(is_live[:, None], hidden[safe_rows], jnp.zeros((), jnp.bfloat16))
    slot_targets = jnp.where(is_live, targets[safe_rows], -1)
    arrived = lax.all_to_all(
        pieces.reshape(groups, capacity, pieces.shape[1]),
        "grp",
        split_axis=0,
        concat_axis=0,
        tiled=True,
    )
    full_rows = lax.all_gather(
        arrived.reshape(shard_rows, pieces.shape[1]), "vocab", axis=1, tiled=True
    )
    block_rows = lax.all_to_all(full_rows, "grp", split_axis=1, concat_axis=0, tiled=True)
    target_ids = lax.all_to_all(
        slot_targets.reshape(groups, capacity), "grp", split_axis=0, concat_axis=0, tiled=True
    ).reshape(shard_rows)
    logits = lax.psum_scatter(
        jnp.dot(block_rows, head, preferred_element_type=jnp.float32),
        "grp",
        scatter_dimension=0,
        tiled=True,
    )
    columns = my_vocab * vocab_dev + jnp.arange(vocab_dev, dtype=jnp.int32)
    row_max, row_total, first_mom, second_mom, target_val = local_stats(
        logits, target_ids, columns, 1
    )
    row_max, row_total, first_mom, second_mom = combined_all(
        (row_max, row_total, first_mom, second_mom), "vocab", combine_stats
    )
    target_val = lax.psum(target_val, "vocab")
    token_scores = final_scores(target_ids, row_max, row_total, first_mom, second_mom, target_val)
    returned = lax.all_to_all(
        token_scores.reshape(groups, capacity), "grp", split_axis=0, concat_axis=0, tiled=True
    ).reshape(shard_rows)
    row_val = (
        jnp.zeros((shard_rows + 1,), jnp.float32)
        .at[jnp.where(is_live, table, shard_rows)]
        .set(returned)[:shard_rows]
    )
    flagged = (flag_col < groups).astype(jnp.float32)
    doc_ends = jnp.cumsum(lengths[0])
    doc_starts = doc_ends - lengths[0]
    positions = jnp.arange(shard_rows, dtype=jnp.int32)
    membership = (
        (positions[None, :] >= doc_starts[:, None]) & (positions[None, :] < doc_ends[:, None])
    ).astype(jnp.float32)
    sums = jnp.sum(membership * row_val[None, :], axis=1)
    counts = jnp.sum(membership * flagged[None, :], axis=1)
    doc_means = (sums / jnp.maximum(counts, 1.0))[None, :]
    return (token_scores, doc_means)


def solution(mesh):
    placed = (P("grp", "vocab"), P("grp", None), P("grp"), P("grp", "vocab"), P("grp", None))
    return jax.shard_map(
        shards, mesh=mesh, in_specs=placed, out_specs=(P("grp"), P("grp", None)), check_vma=False
    )
```

profile of v0, /device:TPU:1, one launch (start us, length us, event | category | flops | bytes accessed | tf_op | source)
XLA Modules:
  0.0 488.9 jit_solution(7191298796290074408)
XLA Ops:
  7.2 0.8 fusion.12
  8.2 0.8 select_reduce_fusion.1
  9.0 0.7 fusion.19
  9.7 1.0 scatter_custom_fusion
  10.8 0.9 gather_fusion.1
  11.7 11.6 %all_to_all.39 = bf16[8,16,512]{2,1,0:T(8,128)(2,1)} all-to-all(bf16[8,16,512]{2,1,0:T(8,128)(2,1)S(1)} %broadcast_select_fusion), channel_id=1, replica_groups=mesh['grp'=8,'vocab'=32] {'grp'}, dimensions={0} | all-to-all | bytes 262144 | tf_op jit(solution)/shard_map/all_to_all | solution.py:79
  23.4 80.8 %all-gather.10.cloned.1.call-done = bf16[128,16384]{1,0:T(8,128)(2,1)} async-done(((bf16[128,512]{1,0:T(8,128)(2,1)}), bf16[128,16384]{1,0:T(8,128)(2,1)}) %all-gather.10.cloned.1.call-update) | async-done | bytes 4194320 | tf_op jit(solution)/shard_map/all_gather | solution.py:86
  104.2 6.4 %copy.16 = bf16[128,16384]{0,1:T(8,128)(2,1)} copy(bf16[128,16384]{1,0:T(8,128)(2,1)} %all-gather.10.cloned.1.call-done) | data formatting | bytes 8388608 | tf_op jit(solution)/shard_map/all_gather | solution.py:86
  110.6 57.6 %all_to_all.40 = bf16[128,8,2048]{0,2,1:T(8,128)(2,1)} all-to-all(bf16[128,8,2048]{0,2,1:T(8,128)(2,1)} %bitcast.91), channel_id=1, replica_groups=mesh['grp'=8,'vocab'=32] {'grp'}, dimensions={1} | all-to-all | bytes 8388608 | tf_op jit(solution)/shard_map/all_to_all | solution.py:89
  168.2 6.5 %copy.17 = bf16[8,128,2048]{2,1,0:T(8,128)(2,1)} copy(bf16[8,128,2048]{1,2,0:T(8,128)(2,1)} %bitcast.92) | data formatting | bytes 8388608 | tf_op jit(solution)/shard_map/all_to_all | solution.py:89
  174.6 14.4 %fusion.21 = f32[1024,2048]{1,0:T(8,128)} fusion(bf16[1024,2048]{1,0:T(8,128)(2,1)} %bitcast.93, bf16[2048,2048]{1,0:T(8,128)(2,1)} %param.10), kind=kOutput, calls=%fused_computation.58 | convolution fusion | flops 8589934592 | bytes 20971520 | tf_op jit(solution)/shard_map/dot_general | solution.py:94
  189.1 0.6 copy-done.1
  189.7 1.2 gather_fusion
  191.0 0.7 select_n.65
  191.6 4.2 all-to-all-start
  196.1 4.4 all-to-all-done
  201.0 0.7 reduce.6
  201.7 40.7 %reduce-scatter.2.cloned.1.call-done = f32[128,2048]{1,0:T(8,128)} async-done(((f32[1024,2048]{1,0:T(8,128)}), f32[128,2048]{1,0:T(8,128)}) %reduce-scatter.2.cloned.1.call-update) | async-done | bytes 1048592 | tf_op jit(solution)/shard_map/reduce_scatter | solution.py:93
  242.4 1.4 reduce_max.9
  243.8 31.7 %all-gather.4 = f32[32,1,128]{2,1,0:T(1,128)S(1)} all-gather(f32[1,1,128]{2,1,0:T(1,128)S(1)} %bitcast.100), channel_id=2, replica_groups=mesh['grp'=8,'vocab'=32] {'vocab'}, dimensions={0}, use_global_device_ids=true | all-gather | bytes 16896 | tf_op jit(solution)/shard_map/all_gather | solution.py:8
  275.4 1.7 fusion.11
  277.2 27.1 %all-gather.5 = f32[32,1,128]{2,1,0:T(1,128)S(1)} all-gather(f32[1,1,128]{2,1,0:T(1,128)S(1)} %bitcast.103), channel_id=3, replica_groups=mesh['grp'=8,'vocab'=32] {'vocab'}, dimensions={0}, use_global_device_ids=true | all-gather | bytes 16896 | tf_op jit(solution)/shard_map/all_gather | solution.py:8
  304.3 28.7 %all-gather.6 = f32[32,1,128]{2,1,0:T(1,128)S(1)} all-gather(f32[1,1,128]{2,1,0:T(1,128)S(1)} %bitcast.102), channel_id=4, replica_groups=mesh['grp'=8,'vocab'=32] {'vocab'}, dimensions={0}, use_global_device_ids=true | all-gather | bytes 16896 | tf_op jit(solution)/shard_map/all_gather | solution.py:8
  333.0 27.2 %all-gather.7 = f32[32,1,128]{2,1,0:T(1,128)S(1)} all-gather(f32[1,1,128]{2,1,0:T(1,128)S(1)} %bitcast.101), channel_id=5, replica_groups=mesh['grp'=8,'vocab'=32] {'vocab'}, dimensions={0}, use_global_device_ids=true | all-gather | bytes 16896 | tf_op jit(solution)/shard_map/all_gather | solution.py:8
  360.2 2.7 while.21
  362.9 56.7 %psum.7 = f32[128]{0:T(128)S(1)} all-reduce(f32[128]{0:T(128)S(1)} %get-tuple-element.232), channel_id=1, replica_groups=mesh['grp'=8,'vocab'=32] {'vocab'}, use_global_device_ids=true, to_apply=%region_5.6 | all-reduce | flops 128 | bytes 1024 | tf_op jit(solution)/shard_map/psum | solution.py:106
  419.6 0.7 all_to_all.33
  420.3 54.2 %all-to-all-start.3 = ((f32[8,1,16]{2,1,0:T(1,128)}), f32[8,1,16]{2,1,0:T(1,128)S(1)}, u32[]{:S(2)}, u32[]{:S(2)}) async-start(f32[8,1,16]{2,1,0:T(1,128)} %bitcast.28), calls=%async_computation.4 | async-start | bytes 8192 | tf_op jit(solution)/shard_map/all_to_all | solution.py:108
  474.5 4.6 all-to-all-done.3
  479.6 0.7 reduce.7
  480.3 1.0 scatter_custom_fusion.1
  481.5 0.5 fusion.18
  (129 shorter events, 3.9 us)
Async XLA Ops:
  7.2 3.6 copy-start
  7.2 97.0 %all-gather.10.cloned.1.call-start = ((), (), s32[]{:S(2)}) async-start(), calls=%async_computation.5 | async-start | bytes 4325376 | tf_op jit(solution)/shard_map/all_gather | solution.py:86
  23.3 219.1 %reduce-scatter.2.cloned.1.call-start = ((), (), s32[]{:S(2)}) async-start(), calls=%async_computation.6 | async-start | bytes 9437184 | tf_op jit(solution)/shard_map/reduce_scatter | solution.py:93
  189.1 0.7 copy-start.1
  189.1 6.8 %copy-start.4 = (s32[1,8]{1,0:T(1,128)S(1)}, s32[1,8]{1,0:T(1,128)}, u32[]{:S(2)}) copy-start(s32[1,8]{1,0:T(1,128)} %param.11) | copy-start | bytes 100
  189.1 285.4 %copy-start.2 = (s32[128,1]{0,1:T(1,128)S(1)}, s32[128,1]{0,1:T(1,128)}, u32[]{:S(2)}) copy-start(s32[128,1]{0,1:T(1,128)} %param.8) | copy-start | bytes 1540
  191.6 8.8 %all-to-all-start = ((s32[8,1,16]{2,1,0:T(1,128)}), s32[8,1,16]{2,1,0:T(1,128)S(1)}, u32[]{:S(2)}, u32[]{:S(2)}) async-start(s32[8,1,16]{2,1,0:T(1,128)} %bitcast.7), calls=%async_computation | async-start | bytes 8192 | tf_op jit(solution)/shard_map/all_to_all | solution.py:90
  419.6 62.5 %copy-start.3 = (f32[128]{0:T(128)}, f32[128]{0:T(128)S(1)}, u32[]{:S(2)}) copy-start(f32[128]{0:T(128)S(1)} %compare_select_fusion.2) | copy-start | bytes 1540
  420.3 58.8 %all-to-all-start.3 = ((f32[8,1,16]{2,1,0:T(1,128)}), f32[8,1,16]{2,1,0:T(1,128)S(1)}, u32[]{:S(2)}, u32[]{:S(2)}) async-start(f32[8,1,16]{2,1,0:T(1,128)} %bitcast.28), calls=%async_computation.4 | async-start | bytes 8192 | tf_op jit(solution)/shard_map/all_to_all | solution.py:108
Sparse Core Ops, SparseCore 0:
  23.4 80.6 all-gather.9
  189.2 53.1 reduce-scatter.1
where the time goes:
time: 490 us; the launch traced here: 489 us
  blocking collectives  241 us (49%)
  waiting for transfers between devices  131 us (27%)
  starting transfers between devices  58.5 us (12%)
  local copies, waits for them, and re-layouts  20.2 us (4%)
  matrix products  14.4 us (3%)
  between operations  14.2 us (3%)
  other arithmetic  9.6 us (2%)
    all_gather x4, blocking collectives, combined_all(): gathered = jax.tree.map(lambda a: lax.all_gather(a, axis), part)  115 us
    all_gather x1, waiting for transfers between devices, shards(): lax.all_gather(arrived.reshape(shard_rows, pieces.shape[1]), 'vocab', axi...  80.8 us
    all_to_all x1, blocking collectives, shards(): lax.all_to_all(full_rows, 'grp', split_axis=1, concat_axis=0, tiled=True)  57.6 us
    psum x1, blocking collectives, shards(): target_val = lax.psum(target_val, 'vocab')  56.7 us
    all_to_all x1, starting transfers between devices, shards(): lax.all_to_all(token_scores.reshape(groups, capacity), 'grp', split_axis=...  54.2 us
    reduce_scatter x1, waiting for transfers between devices, shards(): lax.psum_scatter(jnp.dot(block_rows, head, preferred_element_type=jnp.flo...  40.7 us
    dot_general x1, matrix products, shards(): jnp.dot(block_rows, head, preferred_element_type=jnp.float32)  14.4 us
    all_to_all x1, blocking collectives, shards(): lax.all_to_all(pieces.reshape(groups, capacity, pieces.shape[1]), 'grp',...  11.6 us
  transfers between devices with their start and end apart: 4, of which 4 were waited for; matrix products, arithmetic and copies ran while one was open for 1% of the time, Pallas kernels for 0%

commit v1 on v0

--- a/solution.py
+++ b/solution.py
@@ -103,7 +103,7 @@
     row_max, row_total, first_mom, second_mom = combined_all(
         (row_max, row_total, first_mom, second_mom), "vocab", combine_stats
     )
-    target_val = lax.psum(target_val, "vocab")
+    target_val = jnp.sum(lax.all_gather(target_val, "vocab"), axis=0)
     token_scores = final_scores(target_ids, row_max, row_total, first_mom, second_mom, target_val)
     returned = lax.all_to_all(
         token_scores.reshape(groups, capacity), "grp", split_axis=0, concat_axis=0, tiled=True

time: 490 us -> 455 us (0.929)
  blocking collectives: 241 us -> 212 us
  starting transfers between devices: 58.5 us -> 52.2 us
    psum x1 -> x0, blocking collectives: 56.7 us -> none  [shards(): target_val = lax.psum(target_val, 'vocab')]
    all_gather x0 -> x1, blocking collectives: none -> 28.2 us  [shards(): target_val = jnp.sum(lax.all_gather(target_val, 'vocab'), axis=0)]
    all_to_all x1, starting transfers between devices: 54.2 us -> 47.9 us  [shards(): lax.all_to_all(token_scores.reshape(groups, capacity), 'grp', split_axis=...]
where the time goes in v1:
time: 455 us; the launch traced here: 454 us
  blocking collectives  212 us (47%)
  waiting for transfers between devices  131 us (29%)
  starting transfers between devices  52.2 us (11%)
  local copies, waits for them, and re-layouts  20.2 us (4%)
  matrix products  14.4 us (3%)
  between operations  14.2 us (3%)
  other arithmetic  9.64 us (2%)
    all_gather x4, blocking collectives, combined_all(): gathered = jax.tree.map(lambda a: lax.all_gather(a, axis), part)  115 us
    all_gather x1, waiting for transfers between devices, shards(): lax.all_gather(arrived.reshape(shard_rows, pieces.shape[1]), 'vocab', axi...  80.8 us
    all_to_all x1, blocking collectives, shards(): lax.all_to_all(full_rows, 'grp', split_axis=1, concat_axis=0, tiled=True)  57.6 us
    all_to_all x1, starting transfers between devices, shards(): lax.all_to_all(token_scores.reshape(groups, capacity), 'grp', split_axis=...  47.9 us
    reduce_scatter x1, waiting for transfers between devices, shards(): lax.psum_scatter(jnp.dot(block_rows, head, preferred_element_type=jnp.flo...  40.7 us
    all_gather x1, blocking collectives, shards(): target_val = jnp.sum(lax.all_gather(target_val, 'vocab'), axis=0)  28.2 us
    dot_general x1, matrix products, shards(): jnp.dot(block_rows, head, preferred_element_type=jnp.float32)  14.4 us
    all_to_all x1, blocking collectives, shards(): lax.all_to_all(pieces.reshape(groups, capacity, pieces.shape[1]), 'grp',...  11.6 us
  transfers between devices with their start and end apart: 4, of which 4 were waited for; matrix products, arithmetic and copies ran while one was open for 1% of the time, Pallas kernels for 0%

profile of v1, /device:TPU:1, one launch (start us, length us, event | category | flops | bytes accessed | tf_op | source)
XLA Modules:
  0.0 454.2 jit_solution(16105672444419484942)
XLA Ops:
  7.2 0.8 fusion.12
  8.2 0.8 select_reduce_fusion.1
  9.0 0.7 fusion.19
  9.7 1.0 scatter_custom_fusion
  10.8 0.9 gather_fusion.1
  11.7 11.6 %all_to_all.39 = bf16[8,16,512]{2,1,0:T(8,128)(2,1)} all-to-all(bf16[8,16,512]{2,1,0:T(8,128)(2,1)S(1)} %broadcast_select_fusion), channel_id=1, replica_groups=mesh['grp'=8,'vocab'=32] {'grp'}, dimensions={0} | all-to-all | bytes 262144 | tf_op jit(solution)/shard_map/all_to_all | solution.py:79
  23.4 80.8 %all-gather.12.cloned.1.call-done = bf16[128,16384]{1,0:T(8,128)(2,1)} async-done(((bf16[128,512]{1,0:T(8,128)(2,1)}), bf16[128,16384]{1,0:T(8,128)(2,1)}) %all-gather.12.cloned.1.call-update) | async-done | bytes 4194320 | tf_op jit(solution)/shard_map/all_gather | solution.py:86
  104.2 6.4 %copy.16 = bf16[128,16384]{0,1:T(8,128)(2,1)} copy(bf16[128,16384]{1,0:T(8,128)(2,1)} %all-gather.12.cloned.1.call-done) | data formatting | bytes 8388608 | tf_op jit(solution)/shard_map/all_gather | solution.py:86
  110.6 57.6 %all_to_all.40 = bf16[128,8,2048]{0,2,1:T(8,128)(2,1)} all-to-all(bf16[128,8,2048]{0,2,1:T(8,128)(2,1)} %bitcast.92), channel_id=1, replica_groups=mesh['grp'=8,'vocab'=32] {'grp'}, dimensions={1} | all-to-all | bytes 8388608 | tf_op jit(solution)/shard_map/all_to_all | solution.py:89
  168.2 6.5 %copy.17 = bf16[8,128,2048]{2,1,0:T(8,128)(2,1)} copy(bf16[8,128,2048]{1,2,0:T(8,128)(2,1)} %bitcast.93) | data formatting | bytes 8388608 | tf_op jit(solution)/shard_map/all_to_all | solution.py:89
  174.6 14.4 %fusion.21 = f32[1024,2048]{1,0:T(8,128)} fusion(bf16[1024,2048]{1,0:T(8,128)(2,1)} %bitcast.94, bf16[2048,2048]{1,0:T(8,128)(2,1)} %param.10), kind=kOutput, calls=%fused_computation.58 | convolution fusion | flops 8589934592 | bytes 20971520 | tf_op jit(solution)/shard_map/dot_general | solution.py:94
  189.1 0.6 copy-done.1
  189.7 1.2 gather_fusion
  191.0 0.7 select_n.65
  191.6 4.2 all-to-all-start
  196.1 4.4 all-to-all-done
  201.0 0.7 reduce.7
  201.7 40.7 %reduce-scatter.2.cloned.1.call-done = f32[128,2048]{1,0:T(8,128)} async-done(((f32[1024,2048]{1,0:T(8,128)}), f32[128,2048]{1,0:T(8,128)}) %reduce-scatter.2.cloned.1.call-update) | async-done | bytes 1048592 | tf_op jit(solution)/shard_map/reduce_scatter | solution.py:93
  242.4 1.4 reduce_max.9
  243.8 31.7 %all-gather.6 = f32[32,1,128]{2,1,0:T(1,128)S(1)} all-gather(f32[1,1,128]{2,1,0:T(1,128)S(1)} %bitcast.101), channel_id=3, replica_groups=mesh['grp'=8,'vocab'=32] {'vocab'}, dimensions={0}, use_global_device_ids=true | all-gather | bytes 16896 | tf_op jit(solution)/shard_map/all_gather | solution.py:8
  275.4 1.7 fusion.11
  277.2 27.1 %all-gather.7 = f32[32,1,128]{2,1,0:T(1,128)S(1)} all-gather(f32[1,1,128]{2,1,0:T(1,128)S(1)} %bitcast.105), channel_id=4, replica_groups=mesh['grp'=8,'vocab'=32] {'vocab'}, dimensions={0}, use_global_device_ids=true | all-gather | bytes 16896 | tf_op jit(solution)/shard_map/all_gather | solution.py:8
  304.3 28.7 %all-gather.8 = f32[32,1,128]{2,1,0:T(1,128)S(1)} all-gather(f32[1,1,128]{2,1,0:T(1,128)S(1)} %bitcast.104), channel_id=5, replica_groups=mesh['grp'=8,'vocab'=32] {'vocab'}, dimensions={0}, use_global_device_ids=true | all-gather | bytes 16896 | tf_op jit(solution)/shard_map/all_gather | solution.py:8
  333.0 27.2 %all-gather.9 = f32[32,1,128]{2,1,0:T(1,128)S(1)} all-gather(f32[1,1,128]{2,1,0:T(1,128)S(1)} %bitcast.103), channel_id=6, replica_groups=mesh['grp'=8,'vocab'=32] {'vocab'}, dimensions={0}, use_global_device_ids=true | all-gather | bytes 16896 | tf_op jit(solution)/shard_map/all_gather | solution.py:8
  360.2 2.7 while.21
  362.9 28.2 %all-gather.5 = f32[32,1,128]{2,1,0:T(1,128)S(1)} all-gather(f32[1,1,128]{2,1,0:T(1,128)S(1)} %bitcast.102), channel_id=2, replica_groups=mesh['grp'=8,'vocab'=32] {'vocab'}, dimensions={0}, use_global_device_ids=true | all-gather | bytes 16896 | tf_op jit(solution)/shard_map/all_gather | solution.py:106
  391.2 0.7 all_to_all.33
  391.9 47.9 %all-to-all-start.3 = ((f32[8,1,16]{2,1,0:T(1,128)}), f32[8,1,16]{2,1,0:T(1,128)S(1)}, u32[]{:S(2)}, u32[]{:S(2)}) async-start(f32[8,1,16]{2,1,0:T(1,128)} %bitcast.29), calls=%async_computation.4 | async-start | bytes 8192 | tf_op jit(solution)/shard_map/all_to_all | solution.py:108
  439.8 4.6 %all-to-all-done.3 = f32[8,1,16]{2,1,0:T(1,128)S(1)} async-done(((f32[8,1,16]{2,1,0:T(1,128)}), f32[8,1,16]{2,1,0:T(1,128)S(1)}, u32[]{:S(2)}, u32[]{:S(2)}) %all-to-all-start.3) | async-done | bytes 544 | tf_op jit(solution)/shard_map/all_to_all | solution.py:108
  444.9 0.7 reduce.8
  445.6 1.0 scatter_custom_fusion.1
  446.8 0.5 fusion.18
  (130 shorter events, 3.9 us)
Async XLA Ops:
  7.2 3.6 copy-start
  7.2 97.0 %all-gather.12.cloned.1.call-start = ((), (), s32[]{:S(2)}) async-start(), calls=%async_computation.5 | async-start | bytes 4325376 | tf_op jit(solution)/shard_map/all_gather | solution.py:86
  23.3 219.1 %reduce-scatter.2.cloned.1.call-start = ((), (), s32[]{:S(2)}) async-start(), calls=%async_computation.6 | async-start | bytes 9437184 | tf_op jit(solution)/shard_map/reduce_scatter | solution.py:93
  189.1 0.7 copy-start.1
  189.1 6.8 %copy-start.4 = (s32[1,8]{1,0:T(1,128)S(1)}, s32[1,8]{1,0:T(1,128)}, u32[]{:S(2)}) copy-start(s32[1,8]{1,0:T(1,128)} %param.11) | copy-start | bytes 100
  189.1 250.7 %copy-start.2 = (s32[128,1]{0,1:T(1,128)S(1)}, s32[128,1]{0,1:T(1,128)}, u32[]{:S(2)}) copy-start(s32[128,1]{0,1:T(1,128)} %param.8) | copy-start | bytes 1540
  191.6 8.8 %all-to-all-start = ((s32[8,1,16]{2,1,0:T(1,128)}), s32[8,1,16]{2,1,0:T(1,128)S(1)}, u32[]{:S(2)}, u32[]{:S(2)}) async-start(s32[8,1,16]{2,1,0:T(1,128)} %bitcast.7), calls=%async_computation | async-start | bytes 8192 | tf_op jit(solution)/shard_map/all_to_all | solution.py:90
  391.2 56.2 %copy-start.3 = (f32[128]{0:T(128)}, f32[128]{0:T(128)S(1)}, u32[]{:S(2)}) copy-start(f32[128]{0:T(128)S(1)} %compare_select_fusion.2) | copy-start | bytes 1540
  391.9 52.5 %all-to-all-start.3 = ((f32[8,1,16]{2,1,0:T(1,128)}), f32[8,1,16]{2,1,0:T(1,128)S(1)}, u32[]{:S(2)}, u32[]{:S(2)}) async-start(f32[8,1,16]{2,1,0:T(1,128)} %bitcast.29), calls=%async_computation.4 | async-start | bytes 8192 | tf_op jit(solution)/shard_map/all_to_all | solution.py:108
Sparse Core Ops, SparseCore 0:
  23.4 80.6 all-gather.11
  189.2 53.1 reduce-scatter.1
